TPU v7x, 256 devices: a whole 4x4x8 slice. The times are simulated.
256 devices in a mesh: ctx: 32 (over z, x), dp: 8 (over y, core).
Axes of the slice: x: 4, y: 4, z: 8, core: 2. Of those that a mesh axis runs over, the one named last changes fastest.
Arguments:
- query: bfloat16 [8, 32, 2, 64, 4096], P('dp', 'ctx'), may hold values from -42 to 42, as said below
- key: bfloat16 [8, 32, 2, 64, 1024], P('dp', 'ctx'), may hold values from -4 to 4, as said below
- value: bfloat16 [8, 32, 2, 64, 1024], P('dp', 'ctx'), may hold values from -6 to 6
- beacon_slot_state: bfloat16 [8, 32, 2, 8, 4096], P('dp', 'ctx'), may hold values from -6 to 6
- frozen_beacon_cache: bfloat16 [8, 32, 2, 8, 2048], P('dp', 'ctx'), may hold values from -6 to 6
- adapter_down_weight: bfloat16 [4096, 64], replicated, may hold values from -0.09375 to 0.09375
- adapter_up_weight: bfloat16 [64, 2048], replicated, may hold values from -0.75 to 0.75
- output_cotangent: bfloat16 [8, 32, 2, 64, 4096], P('dp', 'ctx'), may hold values from -6 to 6
- span_beacon_count: int32 [8, 32, 2], P('dp', 'ctx'), may hold values from 1 to 8, as said below
- span_document: int32 [8, 32, 2], P('dp', 'ctx'), may hold values from 0 to 4, as said below
- boundary: int32 [8, 32, 2], P('dp', 'ctx'), may hold values from 1 to 64, as said below
Outputs:
- attended: bfloat16 [8, 32, 2, 64, 4096], P('dp', 'ctx')
- grad_query: bfloat16 [8, 32, 2, 64, 4096], P('dp', 'ctx')
- grad_key: bfloat16 [8, 32, 2, 64, 1024], P('dp', 'ctx')
- grad_value: bfloat16 [8, 32, 2, 64, 1024], P('dp', 'ctx')
- beacon_cache_gradient: bfloat16 [8, 32, 2, 8, 2048], P('dp', 'ctx')
- adapter_gradient: float32 [64, 6144], replicated
Inputs may be any that keep to these rules, and one draw needn't show every extreme that they name: `span_beacon_count`: the two spans of one pair index hold at most 12 beacons together; in every sequence one pair holds exactly 8 and 4. `span_document`: document numbers start at 0 in span 0 and rise by 0 or 1 from span c to span c + 1 in natural span order; every sequence reaches the largest. Every span that is not the last of its document has boundary 64. `query`: queries are real values. `key`: keys are real values.
All inputs are finite; a program needn't handle non-finite values.
Results may differ from a plain program's by a relative error of at most 0.02.
Values may be sent and summed in bfloat16 or wider, within the bound.
No kernel may reach another device: no remote copies, remote signals or barrier semaphores. Data moves between devices by JAX's collectives and lax.ppermute only.
A program may use at most 128 MiB of HBM per device.

v0:
```python
import jax
import jax.numpy as jnp
from jax import lax
from jax.sharding import PartitionSpec as P

MODEL_WIDTH = 4096
KVH = 8
HD = 128
SPAN = 64
MAX_BEACONS = 8
GROUP = 4
QW = 4096
KEY_FEATURES = 1024
masked_score = -1e30


def attend(
    query,
    key,
    value,
    output_cotangent,
    beacon_states,
    own_span,
    own_doc,
    live_lengths,
    slot_span,
    slot_doc,
):
    score_scale = HD ** (-0.5)
    positions = jnp.arange(SPAN)
    live_rows = positions[None, :] < live_lengths[:, None]
    near_mask = (positions[None, None, :] <= positions[None, :, None]) & (
        live_rows[:, :, None] == live_rows[:, None, :]
    )
    far_mask = (
        live_rows[:, :, None]
        & (slot_span[None, None, :] < own_span[:, None, None])
        & (slot_doc[None, None, :] == own_doc[:, None, None])
    )
    visible = jnp.concatenate([near_mask, far_mask], axis=2)[:, None, None]
    query_heads = query.reshape(2, SPAN, KVH, GROUP, HD)
    key_heads = key.reshape(2, SPAN, KVH, HD)
    value_heads = value.reshape(2, SPAN, KVH, HD)
    grad_heads = output_cotangent.reshape(2, SPAN, KVH, GROUP, HD)
    beacon_keys = beacon_states[:, :KEY_FEATURES].reshape(-1, KVH, HD)
    beacon_values = beacon_states[:, KEY_FEATURES:].reshape(-1, KVH, HD)
    scores = (
        jnp.concatenate(
            [
                jnp.einsum(
                    "sqgmd,skgd->sgmqk", query_heads, key_heads, preferred_element_type=jnp.float32
                ),
                jnp.einsum(
                    "sqgmd,kgd->sgmqk", query_heads, beacon_keys, preferred_element_type=jnp.float32
                ),
            ],
            axis=4,
        )
        * score_scale
    )
    scores = jnp.where(visible, scores, masked_score)
    row_max = jnp.max(scores, axis=4, keepdims=True)
    log_total = row_max + jnp.log(jnp.sum(jnp.exp(scores - row_max), axis=4, keepdims=True))
    probs_exact = jnp.exp(scores - log_total)
    probs = probs_exact.astype(jnp.bfloat16)
    near_probs = probs[..., :SPAN]
    far_probs = probs[..., SPAN:]
    summed = jnp.einsum(
        "sgmqk,skgd->sqgmd", near_probs, value_heads, preferred_element_type=jnp.float32
    ) + jnp.einsum("sgmqk,kgd->sqgmd", far_probs, beacon_values, preferred_element_type=jnp.float32)
    attended = summed.astype(jnp.bfloat16)
    attended_heads = lax.optimization_barrier(attended).astype(jnp.float32)
    row_delta = jnp.transpose(
        jnp.sum(grad_heads.astype(jnp.float32) * attended_heads, axis=4), (0, 2, 3, 1)
    )[..., None]
    grad_probs = jnp.concatenate(
        [
            jnp.einsum(
                "sqgmd,skgd->sgmqk", grad_heads, value_heads, preferred_element_type=jnp.float32
            ),
            jnp.einsum(
                "sqgmd,kgd->sgmqk", grad_heads, beacon_values, preferred_element_type=jnp.float32
            ),
        ],
        axis=4,
    )
    grad_scores = (probs_exact * (grad_probs - row_delta)).astype(jnp.bfloat16)
    near_grads = grad_scores[..., :SPAN]
    far_grads = grad_scores[..., SPAN:]
    grad_query = (
        jnp.einsum("sgmqk,skgd->sqgmd", near_grads, key_heads, preferred_element_type=jnp.float32)
        + jnp.einsum("sgmqk,kgd->sqgmd", far_grads, beacon_keys, preferred_element_type=jnp.float32)
    ) * score_scale
    grad_key = (
        jnp.einsum("sgmqk,sqgmd->skgd", near_grads, query_heads, preferred_element_type=jnp.float32)
        * score_scale
    )
    grad_value = jnp.einsum(
        "sgmqk,sqgmd->skgd", near_probs, grad_heads, preferred_element_type=jnp.float32
    )
    result_list = (
        attended.reshape(2, SPAN, QW),
        grad_query.astype(jnp.bfloat16).reshape(2, SPAN, QW),
        grad_key.astype(jnp.bfloat16).reshape(2, SPAN, KEY_FEATURES),
        grad_value.astype(jnp.bfloat16).reshape(2, SPAN, KEY_FEATURES),
    )
    return (result_list, far_grads, far_probs, query_heads, grad_heads)


def local(
    query,
    key,
    value,
    beacon_slot_state,
    frozen_beacon_cache,
    adapter_down_weight,
    adapter_up_weight,
    output_cotangent,
    span_beacon_count,
    span_document,
    boundary,
):
    pair_count = lax.axis_size("ctx")
    device_index = lax.axis_index("ctx")
    own_span = jnp.stack([device_index, 2 * pair_count - 1 - device_index])
    counts = span_beacon_count[0, 0]
    doc_ids = span_document[0, 0]
    live_lengths = boundary[0, 0]
    flattened_state = beacon_slot_state[0, 0].reshape(2 * MAX_BEACONS, MODEL_WIDTH)
    reduced_state = jnp.dot(
        flattened_state, adapter_down_weight, preferred_element_type=jnp.float32
    ).astype(jnp.bfloat16)
    states = (
        frozen_beacon_cache[0, 0].reshape(2 * MAX_BEACONS, 2 * KEY_FEATURES)
        + jnp.dot(reduced_state, adapter_up_weight, preferred_element_type=jnp.float32)
    ).astype(jnp.bfloat16)
    slot_ids = jnp.arange(2 * MAX_BEACONS)
    which_side = slot_ids // MAX_BEACONS
    valid_slots = slot_ids % MAX_BEACONS < counts[which_side]
    send_span = own_span[which_side]
    send_doc = jnp.where(valid_slots, doc_ids[which_side], -1)
    slot_rows = states.shape[0]
    gathered, all_spans, all_docs = (
        lax.all_gather(states[None, None], "ctx", axis=1, tiled=True),
        lax.all_gather(send_span[None, None], "ctx", axis=1, tiled=True),
        lax.all_gather(send_doc[None, None], "ctx", axis=1, tiled=True),
    )
    all_states = gathered[0].reshape(-1, 2 * KEY_FEATURES)
    result_list, far_grads, far_probs, query_heads, grad_heads = attend(
        query[0, 0],
        key[0, 0],
        value[0, 0],
        output_cotangent[0, 0],
        all_states,
        own_span,
        doc_ids,
        live_lengths,
        all_spans.reshape(-1),
        all_docs.reshape(-1),
    )
    score_scale = HD ** (-0.5)
    key_part = (
        jnp.einsum("sgmqk,sqgmd->kgd", far_grads, query_heads, preferred_element_type=jnp.float32)
        * score_scale
    )
    value_part = jnp.einsum(
        "sgmqk,sqgmd->kgd", far_probs, grad_heads, preferred_element_type=jnp.float32
    )
    returned_values = lax.psum_scatter(
        jnp.concatenate(
            [
                key_part.reshape(lax.axis_size("ctx") * slot_rows, KEY_FEATURES),
                value_part.reshape(lax.axis_size("ctx") * slot_rows, KEY_FEATURES),
            ],
            axis=1,
        ),
        "ctx",
        scatter_dimension=0,
        tiled=True,
    ).astype(jnp.bfloat16)
    reduced_gradient = jnp.dot(
        returned_values, adapter_up_weight.T, preferred_element_type=jnp.float32
    ).astype(jnp.bfloat16)
    down_factor_piece = jnp.dot(
        reduced_gradient.T, flattened_state, preferred_element_type=jnp.float32
    )
    up_factor_piece = jnp.dot(reduced_state.T, returned_values, preferred_element_type=jnp.float32)
    adapter_gradient = lax.psum(
        jnp.concatenate([down_factor_piece, up_factor_piece], axis=1), ("ctx", "dp")
    )
    attended, grad_query, grad_key, grad_value = result_list
    return (
        attended[None, None],
        grad_query[None, None],
        grad_key[None, None],
        grad_value[None, None],
        returned_values.reshape(1, 1, 2, MAX_BEACONS, 2 * KEY_FEATURES),
        adapter_gradient,
    )


def solution(mesh):
    return jax.shard_map(
        local,
        mesh=mesh,
        in_specs=(
            P("dp", "ctx", None, None, None),
            P("dp", "ctx", None, None, None),
            P("dp", "ctx", None, None, None),
            P("dp", "ctx", None, None, None),
            P("dp", "ctx", None, None, None),
            P(),
            P(),
            P("dp", "ctx", None, None, None),
            P("dp", "ctx", None),
            P("dp", "ctx", None),
            P("dp", "ctx", None),
        ),
        out_specs=(
            P("dp", "ctx", None, None, None),
            P("dp", "ctx", None, None, None),
            P("dp", "ctx", None, None, None),
            P("dp", "ctx", None, None, None),
            P("dp", "ctx", None, None, None),
            P(),
        ),
        check_vma=False,
    )
```

profile of v0, /device:TPU:2, one launch (start us, length us, event | category | flops | bytes accessed | tf_op | source)
XLA Modules:
  0.0 628.6 jit_solution(4446207362241377549)
XLA Ops:
  7.3 1.0 copy-done
  8.2 1.1 convolution_convert_fusion.1
  9.4 1.8 fusion.12
  11.2 1.3 fusion.59
  12.5 1.3 fusion.60
  13.8 2.6 fusion.54
  16.4 41.4 %all_gather.10 = s32[1,32,16]{2,0,1:T(1,128)S(1)} all-gather(s32[1,1,16]{2,0,1:T(1,128)S(1)} %fusion.54), channel_id=1, replica_groups=mesh['ctx'=32,'dp'=8] {'ctx'}, dimensions={1}, use_global_device_ids=true | all-gather | bytes 2112 | tf_op jit(solution)/shard_map/all_gather | solution.py:146
  58.3 0.7 reduce.3
  59.1 1.0 copy.174
  60.1 1.0 copy.176
  61.1 1.8 reshape_squeeze.24
  62.9 2.6 reshape_squeeze.20
  65.5 0.6 dynamic-slice
  66.9 16.7 %all-reduce = s32[512]{0:T(512)S(1)} all-reduce(s32[512]{0:T(512)S(1)} %bitcast_dynamic-update-slice_fusion), channel_id=4, replica_groups=mesh['ctx'=32,'dp'=8] {'ctx'}, use_global_device_ids=true, to_apply=%add | all-reduce | flops 512 | bytes 4096
  84.3 1.8 convolution_bitcast_fusion.3
  86.2 2.1 convolution_bitcast_fusion.2
  88.2 2.9 all-gather.5.cloned.1.call-done
  91.1 1.8 slice_bitcast_fusion
  93.2 1.3 convolution_bitcast_fusion.1
  94.5 4.3 fusion.28
  98.7 5.0 exponential_reduce_fusion
  103.8 4.0 fusion.3
  108.2 3.3 fusion.8
  111.8 1.3 convolution_bitcast_fusion
  113.1 2.1 fusion.15
  115.2 0.8 multiply_reduce_fusion
  116.0 7.9 %fusion.2 = bf16[2,8,4,64,576]{4,3,2,0,1:T(8,128)(2,1)S(1)} fusion(f32[2,8,4,64,512]{4,3,2,0,1:T(8,128)S(1)} %convolution_bitcast_fusion, f32[2,8,4,64,64]{4,3,2,0,1:T(8,128)S(1)} %copy-done.4, f32[2,8,4,64]{3,2,0,1:T(4,128)S(1)} %bitcast.150, f32[2,8,4,64,512]{4,3,2,0,1:T(8,128)S(1)} %convolution_bitcast_fusion.1, pred[2,64,576]{2,1,0:T(8,128)(4,1)S(1)} %pad_add_fusion, ...), kind=kLoop, calls=%fused_computation.4 | loop fusion | flops 18874368 | bytes 23699456 | tf_op jit(solution)/shard_map/convert_element_type | solution.py:87
  124.0 2.5 bitcast_multiply_fusion
  126.5 0.6 copy-done.13
  127.1 2.4 pad_maximum_fusion
  129.5 5.5 copy.172
  135.1 1.8 copy.117
  136.9 1.9 fusion.26
  139.0 0.8 broadcast_in_dim_reshape.17
  139.8 2.7 broadcast_in_dim_reshape.14
  142.5 1.9 fusion.25
  144.5 0.8 broadcast_in_dim_reshape.16
  145.4 3.1 fusion.35
  148.4 205.6 %reduce-scatter.4.cloned.1.call-done = f32[16,2048]{1,0:T(8,128)} async-done(((f32[512,2048]{1,0:T(8,128)}), f32[16,2048]{1,0:T(8,128)}) %reduce-scatter.4.cloned.1.call-update) | async-done | bytes 131088 | tf_op jit(solution)/shard_map/reduce_scatter | solution.py:169
  354.0 1.1 fusion.55
  355.2 1.5 fusion.27
  356.7 1.3 pad_maximum_fusion.1
  358.0 5.1 fusion.14
  363.2 0.8 copy.128
  364.0 1.6 broadcast_in_dim_reshape.15
  365.6 0.6 convert_bitcast_fusion
  366.2 253.2 %all-reduce.3.cloned.1.call-done = f32[64,6144]{1,0:T(8,128)} async-done(((f32[64,6144]{1,0:T(8,128)}), f32[64,6144]{1,0:T(8,128)}) %all-reduce.3.cloned.1.call-update) | async-done | bytes 1572880 | tf_op jit(solution)/shard_map/psum | solution.py:188
  619.4 2.7 copy.245
  (64 shorter events, 3.0 us)
Async XLA Ops:
  7.2 1.1 copy-start
  7.2 58.3 %copy-start.19 = (u32[256]{0:T(256)S(1)}, u32[256]{0:T(256)}, u32[]{:S(2)}) copy-start(u32[256]{0:T(256)} %constant.71) | copy-start | bytes 3076
  7.2 76.6 %copy-start.17 = (s32[1,1,2]{2,1,0:T(1,128)S(1)}, s32[1,1,2]{2,1,0:T(1,128)}, u32[]{:S(2)}) copy-start(s32[1,1,2]{2,1,0:T(1,128)} %param.20) | copy-start | bytes 28
  7.2 76.5 %copy-start.18 = (s32[1,1,2]{2,1,0:T(1,128)S(1)}, s32[1,1,2]{2,1,0:T(1,128)}, u32[]{:S(2)}) copy-start(s32[1,1,2]{2,1,0:T(1,128)} %param.21) | copy-start | bytes 28
  7.2 83.8 %all-gather.5.cloned.1.call-start = ((), (), s32[]{:S(2)}) async-start(), calls=%async_computation.2 | async-start | bytes 2162688 | tf_op jit(solution)/shard_map/all_gather | solution.py:144
  11.2 342.9 %reduce-scatter.4.cloned.1.call-start = ((), (), s32[]{:S(2)}) async-start(), calls=%async_computation.3 | async-start | bytes 4325376 | tf_op jit(solution)/shard_map/reduce_scatter | solution.py:169
  84.3 1.8 copy-start.11
  91.1 2.1 copy-start.2
  93.2 1.3 copy-start.7
  103.8 4.0 copy-start.12
  107.8 7.4 %copy-start.5 = (bf16[2,8,4,64,576]{4,3,2,0,1:T(8,128)(2,1)}, bf16[2,8,4,64,576]{4,3,2,0,1:T(8,128)(2,1)S(1)}, u32[]{:S(2)}) copy-start(bf16[2,8,4,64,576]{4,3,2,0,1:T(8,128)(2,1)S(1)} %fusion.3) | copy-start | bytes 14155780
  113.1 2.9 copy-start.4
  115.2 8.7 %copy-start.9 = (bf16[2,64,8,4,128]{4,1,3,2,0:T(8,128)(2,1)}, bf16[2,64,8,4,128]{4,1,3,2,0:T(8,128)(2,1)S(1)}, u32[]{:S(2)}) copy-start(bf16[2,64,8,4,128]{4,1,3,2,0:T(8,128)(2,1)S(1)} %fusion.15) | copy-start | bytes 3145732
  124.0 2.5 copy-start.6
  124.0 3.2 copy-start.13
  129.5 5.6 copy-start.10
  135.1 7.4 %copy-start.3 = (bf16[2,64,8,4,128]{4,3,2,1,0:T(4,128)(2,1)S(1)}, bf16[2,64,8,4,128]{4,3,2,1,0:T(4,128)(2,1)}, u32[]{:S(2)}) copy-start(bf16[2,64,8,4,128]{4,3,2,1,0:T(4,128)(2,1)} %reshape_squeeze.20) | copy-start | bytes 3145732
  135.1 484.3 %all-reduce.3.cloned.1.call-start = ((), (), s32[]{:S(2)}) async-start(), calls=%async_computation.1 | async-start | bytes 3145728 | tf_op jit(solution)/shard_map/psum | solution.py:188
  139.8 215.4 %copy-start.15 = (bf16[64,2048]{1,0:T(8,128)(2,1)S(1)}, bf16[64,2048]{1,0:T(8,128)(2,1)}, u32[]{:S(2)}) copy-start(bf16[64,2048]{1,0:T(8,128)(2,1)} %param.17) | copy-start | bytes 786436
  139.8 215.4 %copy-start.16 = (bf16[1,1,2,8,4096]{4,3,2,1,0:T(8,128)(2,1)S(1)}, bf16[1,1,2,8,4096]{4,3,2,1,0:T(8,128)(2,1)}, u32[]{:S(2)}) copy-start(bf16[1,1,2,8,4096]{4,3,2,1,0:T(8,128)(2,1)} %param.14) | copy-start | bytes 393220
  145.4 212.7 %copy-start.8 = (bf16[64,8,8,128]{3,2,1,0:T(8,128)(2,1)S(1)}, bf16[64,8,8,128]{3,2,1,0:T(8,128)(2,1)}, u32[]{:S(2)}) copy-start(bf16[64,8,8,128]{3,2,1,0:T(8,128)(2,1)} %copy-done.7) | copy-start | bytes 3145732
  358.0 7.6 %copy-start.14 = (f32[16,2048]{1,0:T(8,128)S(1)}, f32[16,2048]{1,0:T(8,128)}, u32[]{:S(2)}) copy-start(f32[16,2048]{1,0:T(8,128)} %reduce-scatter.4.cloned.1.call-done) | copy-start | bytes 393220
  358.0 264.0 %copy-start.1 = (bf16[4096,64]{0,1:T(8,128)(2,1)S(1)}, bf16[4096,64]{0,1:T(8,128)(2,1)}, u32[]{:S(2)}) copy-start(bf16[4096,64]{0,1:T(8,128)(2,1)} %param.16) | copy-start | bytes 1572868
Sparse Core Ops, SparseCore 0:
  11.3 79.7 all-gather.4
  135.2 218.8 reduce-scatter.3
  360.8 258.5 all-reduce.2
where the time goes:
time: 629 us
  waiting for transfers between devices  462 us (73%)
  blocking collectives  58.1 us (9%)
  matrix products  32.3 us (5%)
  local copies, waits for them, and re-layouts  31.3 us (5%)
  other arithmetic  30.4 us (5%)
  between operations  14.8 us (2%)
    psum x1, waiting for transfers between devices, local(): lax.psum(jnp.concatenate([down_factor_piece, up_factor_piece], axis=1), (...  253 us
    reduce_scatter x1, waiting for transfers between devices, local(): lax.psum_scatter(jnp.concatenate([key_part.reshape(lax.axis_size('ctx') *...  206 us
    all_gather x1, blocking collectives, local(): lax.all_gather(send_doc[None, None], 'ctx', axis=1, tiled=True)  41.4 us
    unnamed x1, blocking collectives  16.7 us
    unnamed x49, local copies, waits for them, and re-layouts  14.8 us
  transfers between devices with their start and end apart: 3, of which 3 were waited for; matrix products, arithmetic and copies ran while one was open for 6% of the time, Pallas kernels for 0%

commit v1 on v0

--- a/solution.py
+++ b/solution.py
@@ -186,7 +186,7 @@
     )
     up_factor_piece = jnp.dot(reduced_state.T, returned_values, preferred_element_type=jnp.float32)
     adapter_gradient = lax.psum(
-        jnp.concatenate([down_factor_piece, up_factor_piece], axis=1), ("ctx", "dp")
+        lax.psum(jnp.concatenate([down_factor_piece, up_factor_piece], axis=1), "dp"), "ctx"
     )
     attended, grad_query, grad_key, grad_value = result_list
     return (

time: 629 us -> 596 us (0.948)
  waiting for transfers between devices: 462 us -> 424 us
    psum x1 -> x2, waiting for transfers between devices: 253 us -> 202 us  [the longest x1 141 us: local(): lax.psum(lax.psum(jnp.concatenate([down_factor_piece, up_factor_piece], a...]
    reduce_scatter x1, waiting for transfers between devices: 206 us -> 219 us  [local(): lax.psum_scatter(jnp.concatenate([key_part.reshape(lax.axis_size('ctx') *...]
    unnamed x49 -> x47, local copies, waits for them, and re-layouts: 14.8 us -> 14.7 us
  transfers between devices with their start and end apart: 3 -> 4, of which waited for: 3 -> 4; matrix products, arithmetic and copies ran while one was open for 6% -> 6% of each run, Pallas kernels for 0% -> 0%
where the time goes in v1:
time: 596 us; the launch traced here: 594 us
  waiting for transfers between devices  424 us (71%)
  blocking collectives  58.1 us (10%)
  matrix products  34.5 us (6%)
  other arithmetic  31.5 us (5%)
  local copies, waits for them, and re-layouts  31.2 us (5%)
  between operations  14.8 us (2%)
    reduce_scatter x1, waiting for transfers between devices, local(): lax.psum_scatter(jnp.concatenate([key_part.reshape(lax.axis_size('ctx') *...  219 us
    psum x1, waiting for transfers between devices, local(): lax.psum(lax.psum(jnp.concatenate([down_factor_piece, up_factor_piece], a...  141 us
    psum x1, waiting for transfers between devices, local(): lax.psum(jnp.concatenate([down_factor_piece, up_factor_piece], axis=1), '...  61 us
    all_gather x1, blocking collectives, local(): lax.all_gather(send_doc[None, None], 'ctx', axis=1, tiled=True)  41.4 us
    unnamed x1, blocking collectives  16.7 us
    unnamed x47, local copies, waits for them, and re-layouts  14.7 us
  transfers between devices with their start and end apart: 4, of which 4 were waited for; matrix products, arithmetic and copies ran while one was open for 6% of the time, Pallas kernels for 0%

profile of v1, /device:TPU:2, one launch (start us, length us, event | category | flops | bytes accessed | tf_op | source)
XLA Modules:
  0.0 594.5 jit_solution(269394051769954685)
XLA Ops:
  7.3 1.0 copy-done
  8.2 1.1 convolution_convert_fusion.1
  9.4 1.8 fusion.12
  11.2 1.3 fusion.59
  12.5 1.3 fusion.60
  13.8 2.6 fusion.54
  16.4 41.4 %all_gather.10 = s32[1,32,16]{2,0,1:T(1,128)S(1)} all-gather(s32[1,1,16]{2,0,1:T(1,128)S(1)} %fusion.54), channel_id=1, replica_groups=mesh['ctx'=32,'dp'=8] {'ctx'}, dimensions={1}, use_global_device_ids=true | all-gather | bytes 2112 | tf_op jit(solution)/shard_map/all_gather | solution.py:146
  58.3 0.7 reduce.3
  59.1 1.0 copy.174
  60.1 1.0 copy.176
  61.1 1.8 reshape_squeeze.24
  62.9 2.6 reshape_squeeze.20
  66.9 16.7 %all-reduce = s32[512]{0:T(512)S(1)} all-reduce(s32[512]{0:T(512)S(1)} %bitcast_dynamic-update-slice_fusion), channel_id=4, replica_groups=mesh['ctx'=32,'dp'=8] {'ctx'}, use_global_device_ids=true, to_apply=%add | all-reduce | flops 512 | bytes 4096
  84.3 1.8 convolution_bitcast_fusion.3
  86.2 2.1 convolution_bitcast_fusion.2
  88.2 2.8 all-gather.5.cloned.1.call-done
  91.1 1.8 slice_bitcast_fusion
  93.2 1.3 convolution_bitcast_fusion.1
  94.5 4.3 fusion.28
  98.7 5.0 exponential_reduce_fusion
  103.8 4.0 fusion.3
  107.8 2.1 fusion.40
  109.9 3.3 fusion.8
  113.5 1.3 convolution_bitcast_fusion
  114.8 3.8 fusion.15
  118.6 0.8 multiply_reduce_fusion
  119.4 7.9 %fusion.2 = bf16[2,8,4,64,576]{4,3,2,0,1:T(8,128)(2,1)S(1)} fusion(f32[2,8,4,64,512]{4,3,2,0,1:T(8,128)S(1)} %convolution_bitcast_fusion, f32[2,8,4,64,64]{4,3,2,0,1:T(8,128)S(1)} %copy-done.4, f32[2,8,4,64]{3,2,0,1:T(4,128)S(1)} %bitcast.150, f32[2,8,4,64,512]{4,3,2,0,1:T(8,128)S(1)} %convolution_bitcast_fusion.1, pred[2,64,576]{2,1,0:T(8,128)(4,1)S(1)} %pad_add_fusion, ...), kind=kLoop, calls=%fused_computation.4 | loop fusion | flops 18874368 | bytes 23699456 | tf_op jit(solution)/shard_map/convert_element_type | solution.py:87
  127.4 2.5 bitcast_multiply_fusion
  129.9 0.6 copy-done.13
  130.5 2.4 pad_maximum_fusion
  132.9 5.4 copy.172
  138.4 219.0 %reduce-scatter.4.cloned.1.call-done = f32[16,2048]{1,0:T(8,128)} async-done(((f32[512,2048]{1,0:T(8,128)}), f32[16,2048]{1,0:T(8,128)}) %reduce-scatter.4.cloned.1.call-update) | async-done | bytes 131088 | tf_op jit(solution)/shard_map/reduce_scatter | solution.py:169
  357.4 2.0 fusion.55
  359.3 1.6 fusion.27
  361.0 2.3 pad_maximum_fusion.1
  363.4 1.8 copy.117
  365.2 1.9 fusion.26
  367.3 0.8 broadcast_in_dim_reshape.17
  368.1 2.6 broadcast_in_dim_reshape.14
  370.7 61.0 %all-reduce.4.cloned.1.call-done = f32[64,6144]{1,0:T(8,128)} async-done(((f32[64,6144]{1,0:T(8,128)}), f32[64,6144]{1,0:T(8,128)}) %all-reduce.4.cloned.1.call-update) | async-done | bytes 1572880 | tf_op jit(solution)/shard_map/psum | solution.py:189
  431.8 1.9 fusion.25
  433.8 0.8 broadcast_in_dim_reshape.16
  434.7 1.6 fusion.35
  436.3 4.5 fusion.14
  440.9 0.8 copy.128
  441.7 1.6 broadcast_in_dim_reshape.15
  443.9 141.4 %all-reduce.6.cloned.1.call-done = f32[64,6144]{1,0:T(8,128)} async-done(((f32[64,6144]{1,0:T(8,128)}), f32[64,6144]{1,0:T(8,128)}) %all-reduce.6.cloned.1.call-update) | async-done | bytes 1572880 | tf_op jit(solution)/shard_map/psum | solution.py:188
  585.3 2.7 copy.246
  (65 shorter events, 3.8 us)
Async XLA Ops:
  7.2 1.1 copy-start
  7.2 58.3 %copy-start.18 = (u32[256]{0:T(256)S(1)}, u32[256]{0:T(256)}, u32[]{:S(2)}) copy-start(u32[256]{0:T(256)} %constant.71) | copy-start | bytes 3076
  7.2 76.6 %copy-start.16 = (s32[1,1,2]{2,1,0:T(1,128)S(1)}, s32[1,1,2]{2,1,0:T(1,128)}, u32[]{:S(2)}) copy-start(s32[1,1,2]{2,1,0:T(1,128)} %param.20) | copy-start | bytes 28
  7.2 76.5 %copy-start.17 = (s32[1,1,2]{2,1,0:T(1,128)S(1)}, s32[1,1,2]{2,1,0:T(1,128)}, u32[]{:S(2)}) copy-start(s32[1,1,2]{2,1,0:T(1,128)} %param.21) | copy-start | bytes 28
  7.2 83.8 %all-gather.5.cloned.1.call-start = ((), (), s32[]{:S(2)}) async-start(), calls=%async_computation.3 | async-start | bytes 2162688 | tf_op jit(solution)/shard_map/all_gather | solution.py:144
  11.2 346.2 %reduce-scatter.4.cloned.1.call-start = ((), (), s32[]{:S(2)}) async-start(), calls=%async_computation.4 | async-start | bytes 4325376 | tf_op jit(solution)/shard_map/reduce_scatter | solution.py:169
  84.3 1.8 copy-start.11
  91.1 2.1 copy-start.2
  93.2 1.3 copy-start.7
  103.8 4.0 copy-start.12
  107.8 7.0 %copy-start.5 = (bf16[2,8,4,64,576]{4,3,2,0,1:T(8,128)(2,1)}, bf16[2,8,4,64,576]{4,3,2,0,1:T(8,128)(2,1)S(1)}, u32[]{:S(2)}) copy-start(bf16[2,8,4,64,576]{4,3,2,0,1:T(8,128)(2,1)S(1)} %fusion.3) | copy-start | bytes 14155780
  114.8 4.7 copy-start.4
  118.6 8.8 %copy-start.9 = (bf16[2,64,8,4,128]{4,1,3,2,0:T(8,128)(2,1)}, bf16[2,64,8,4,128]{4,1,3,2,0:T(8,128)(2,1)S(1)}, u32[]{:S(2)}) copy-start(bf16[2,64,8,4,128]{4,1,3,2,0:T(8,128)(2,1)S(1)} %fusion.15) | copy-start | bytes 3145732
  127.4 2.5 copy-start.6
  127.4 3.2 copy-start.13
  132.9 226.4 %copy-start.15 = (bf16[1,1,2,8,4096]{4,3,2,1,0:T(8,128)(2,1)S(1)}, bf16[1,1,2,8,4096]{4,3,2,1,0:T(8,128)(2,1)}, u32[]{:S(2)}) copy-start(bf16[1,1,2,8,4096]{4,3,2,1,0:T(8,128)(2,1)} %param.14) | copy-start | bytes 393220
  138.3 225.0 %copy-start.10 = (bf16[2,64,8,4,128]{4,1,3,2,0:T(8,128)(2,1)S(1)}, bf16[2,64,8,4,128]{4,1,3,2,0:T(8,128)(2,1)}, u32[]{:S(2)}) copy-start(bf16[2,64,8,4,128]{4,1,3,2,0:T(8,128)(2,1)} %copy-done.9) | copy-start | bytes 3145732
  138.4 293.4 %all-reduce.4.cloned.1.call-start = ((), (), s32[]{:S(2)}) async-start(), calls=%async_computation.1 | async-start | bytes 3145728 | tf_op jit(solution)/shard_map/psum | solution.py:189
  363.3 68.4 %copy-start.3 = (bf16[2,64,8,4,128]{4,3,2,1,0:T(4,128)(2,1)S(1)}, bf16[2,64,8,4,128]{4,3,2,1,0:T(4,128)(2,1)}, u32[]{:S(2)}) copy-start(bf16[2,64,8,4,128]{4,3,2,1,0:T(4,128)(2,1)} %reshape_squeeze.20) | copy-start | bytes 3145732
  363.3 222.0 %all-reduce.6.cloned.1.call-start = ((), (), s32[]{:S(2)}) async-start(), calls=%async_computation.2 | async-start | bytes 3145728 | tf_op jit(solution)/shard_map/psum | solution.py:188
  370.7 65.6 %copy-start.8 = (bf16[64,8,8,128]{3,2,1,0:T(8,128)(2,1)S(1)}, bf16[64,8,8,128]{3,2,1,0:T(8,128)(2,1)}, u32[]{:S(2)}) copy-start(bf16[64,8,8,128]{3,2,1,0:T(8,128)(2,1)} %copy-done.7) | copy-start | bytes 3145732
  436.3 7.0 %copy-start.14 = (f32[16,2048]{1,0:T(8,128)S(1)}, f32[16,2048]{1,0:T(8,128)}, u32[]{:S(2)}) copy-start(f32[16,2048]{1,0:T(8,128)} %reduce-scatter.4.cloned.1.call-done) | copy-start | bytes 393220
  436.3 151.6 %copy-start.1 = (bf16[4096,64]{0,1:T(8,128)(2,1)S(1)}, bf16[4096,64]{0,1:T(8,128)(2,1)}, u32[]{:S(2)}) copy-start(bf16[4096,64]{0,1:T(8,128)(2,1)} %param.16) | copy-start | bytes 1572868
Sparse Core Ops, SparseCore 0:
  11.3 79.7 all-gather.4
  138.5 218.8 reduce-scatter.3
  363.4 68.2 all-reduce.3
  435.4 149.8 all-reduce.5
